TPU v7x, 128 devices: a whole 4x4x4 slice. The times are simulated.
128 devices in a mesh: tm: 8 (over z, x_hi), docs: 16 (over y, x_lo, core).
Axes of the slice: x: 4 (x_hi: 2, x_lo: 2; x = x_hi * 2 + x_lo), y: 4, z: 4, core: 2. Of those that a mesh axis runs over, the one named last changes fastest.
Arguments:
- counts: int32 [8, 1024, 32768], P('tm', 'docs'), may hold values from 0 to 5, as said below
- topic_means: float32 [8, 32768, 128], P('tm', 'docs'), may hold values from -80 to 170
- doc_topics_init: float32 [8, 1024, 128], P('tm', 'docs'), may hold values from 0.5 to 20
- dirichlet_prior: float32 [128], replicated, may hold values from 0.05 to 1
- chain_var: float32 [128], replicated, may hold values from 0.005 to 0.5
- obs_noise: float32 [128], replicated, may hold values from 0.1 to 10
Outputs:
- smoothed_means: float32 [8, 32768, 128], P('tm', 'docs')
- doc_topics: float32 [8, 1024, 128], P('tm', 'docs')
Inputs may be any that keep to these rules, and one draw needn't show every extreme that they name: `counts`: each entry is 0 or a count of 1 to 5; each word has its own share of nonzero entries, between a quarter and three quarters.
All inputs are finite; a program needn't handle non-finite values.
Results may differ from a plain program's by a relative error of at most 0.01.
Values may be sent and summed in bfloat16 or wider, within the bound.
No kernel may reach another device: no remote copies, remote signals or barrier semaphores. Data moves between devices by JAX's collectives and lax.ppermute only.
A program may use at most 128 MiB of HBM per device.

v0:
```python
import jax
import jax.numpy as jnp
from jax import lax
from jax.sharding import Mesh
from jax.sharding import PartitionSpec as P

V = 32768
ITERS_E = 4
TM = ("tm_0", "tm_1")
TM_DOCS = ("tm_0", "tm_1", "docs")
prior_count = 0.5
initial_scale = 1000.0


def merged(part, axis, combine):
    gathered = jax.tree.map(lambda a: lax.all_gather(a, axis), part)

    def take(source):
        return jax.tree.map(lambda a: lax.dynamic_index_in_dim(a, source, 0, False), gathered)

    return lax.fori_loop(
        1, lax.axis_size(axis), lambda source, state: combine(state, take(source)), take(0)
    )


def filled_with(shard, identity):
    return jax.tree.map(
        lambda a, e: jnp.broadcast_to(jnp.asarray(e, a.dtype), a.shape), shard, identity
    )


def carried_in(shard, axes, combine, identity):
    before = start = filled_with(shard, identity)
    subtotal = shard
    for axis in reversed(axes):
        devices, place = (lax.axis_size(axis), lax.axis_index(axis))
        pieces = jax.tree.map(
            lambda part, kind: lax.all_gather(part.astype(kind), axis),
            subtotal,
            (jnp.bfloat16, jnp.bfloat16),
        )
        inside, subtotal = (start, start)
        for k in range(devices):
            passed = k < place
            subtotal = combine(
                subtotal, jax.tree.map(lambda part, own: part[k].astype(own.dtype), pieces, shard)
            )
            inside = jax.tree.map(lambda new, old: jnp.where(passed, new, old), subtotal, inside)
        before = combine(inside, before)
    return before


def prefix_by_axis(shard, axes, combine, identity):
    before = start = filled_with(shard, identity)
    subtotal = shard
    for axis in reversed(axes):
        devices, place = (lax.axis_size(axis), lax.axis_index(axis))
        pieces = jax.tree.map(
            lambda part, kind: lax.all_gather(part.astype(kind), axis),
            subtotal,
            jax.tree.map(lambda a: jnp.bfloat16 if a.dtype == jnp.float32 else a.dtype, shard),
        )
        inside, subtotal = (start, start)
        for k in reversed(range(devices)):
            passed = k > place
            subtotal = combine(
                subtotal, jax.tree.map(lambda part, own: part[k].astype(own.dtype), pieces, shard)
            )
            inside = jax.tree.map(lambda new, old: jnp.where(passed, new, old), subtotal, inside)
        before = combine(inside, before)
    return before


def chain_factors(totals, chain_var, obs_noise):
    relative = jnp.sum(totals, axis=1, keepdims=True) / (totals.shape[1] * totals)
    noise = obs_noise[None, :] * relative

    def advance(previous, noise_level):
        predicted = previous + chain_var
        own_gain = predicted / (predicted + noise_level)
        current = (1.0 - own_gain) * predicted
        return (current, (own_gain, current))

    unused, (gains, filtered_var) = lax.scan(advance, initial_scale * chain_var, noise)
    smooth = filtered_var / (filtered_var + chain_var)
    smooth = jnp.concatenate([smooth[:-1], jnp.zeros_like(smooth[-1:])], axis=0)
    return (gains, smooth)


def compose(former, latter):
    return (former[0] * latter[0], latter[0] * former[1] + latter[1])


def join_mass(former, latter):
    highest = jnp.maximum(former[0], latter[0])
    return (
        highest,
        former[1] * jnp.exp(former[0] - highest) + latter[1] * jnp.exp(latter[0] - highest),
    )


def body(counts, topic_means, doc_topics_init, dirichlet_prior, chain_var, obs_noise):
    topic_slab = topic_means[0]
    concentration = doc_topics_init[0]
    count_wide = counts[0].astype(jnp.float32)
    local_peak = jnp.max(topic_slab, axis=0)
    local_mass = jnp.sum(jnp.exp(topic_slab - local_peak[None, :]), axis=0)
    column_peak, column_mass = merged((local_peak, local_mass), "docs", join_mass)
    beta_slab = jnp.exp(topic_slab - (column_peak + jnp.log(column_mass))[None, :]).astype(
        jnp.bfloat16
    )
    beta_full = lax.all_gather(beta_slab, "docs", axis=0, tiled=True)
    for sweep_index in range(ITERS_E):
        proportions = jnp.exp(lax.digamma(concentration)).astype(jnp.bfloat16)
        mixture = lax.dot_general(
            proportions, beta_full, (((1,), (1,)), ((), ())), preferred_element_type=jnp.float32
        )
        ratios = (count_wide / mixture).astype(jnp.bfloat16)
        update = proportions.astype(jnp.float32) * jnp.dot(
            ratios, beta_full, preferred_element_type=jnp.float32
        )
        concentration = dirichlet_prior[None, :] + update
    word_stats = lax.psum_scatter(
        (
            beta_full.astype(jnp.float32)
            * lax.dot_general(
                ratios, proportions, (((0,), (0,)), ((), ())), preferred_element_type=jnp.float32
            )
        ).astype(jnp.bfloat16),
        "docs",
        scatter_dimension=0,
        tiled=True,
    ).astype(jnp.float32)
    slice_index = lax.axis_index(TM)
    slices = lax.axis_size(TM)
    own_row = (jnp.arange(slices) == slice_index).astype(jnp.float32)
    placed = own_row[:, None] * jnp.sum(update, axis=0)[None, :]
    totals = lax.psum(placed, TM_DOCS)
    gains, smooth = chain_factors(totals, chain_var, obs_noise)
    own_total = jnp.sum(own_row[:, None] * totals, axis=0)
    own_gain = jnp.sum(own_row[:, None] * gains, axis=0)
    own_factor = jnp.sum(own_row[:, None] * smooth, axis=0)
    pseudo = jnp.log(word_stats + prior_count) - jnp.log((own_total + prior_count * V) / V)[None, :]
    forward_rate = 1.0 - own_gain
    forward_term = own_gain[None, :] * pseudo
    neutral = (jnp.ones_like(forward_rate), jnp.zeros_like(forward_term))
    entering = carried_in((forward_rate, forward_term), TM, compose, neutral)[1]
    filtered = forward_rate[None, :] * entering + forward_term
    back_term = (1.0 - own_factor)[None, :] * filtered
    following = prefix_by_axis((own_factor, back_term), TM, compose, neutral)[1]
    smoothed = own_factor[None, :] * following + back_term
    return (smoothed[None], concentration[None])


def solution(mesh):
    split = Mesh(mesh.devices.reshape(4, 2, mesh.shape["docs"]), ("tm_0", "tm_1", "docs"))
    placed = (P(TM, "docs", None), P(TM, "docs", None), P(TM, "docs", None), P(), P(), P())
    return jax.shard_map(
        body,
        mesh=split,
        in_specs=placed,
        out_specs=(P(TM, "docs", None), P(TM, "docs", None)),
        check_vma=False,
    )
```

profile of v0, /device:TPU:1, one launch (start us, length us, event | category | flops | bytes accessed | tf_op | source)
XLA Modules:
  0.0 390.9 jit_solution(17476896300496999206)
XLA Ops:
  7.2 1.5 reduce_max.9
  8.7 1.5 fusion.51
  10.2 21.2 %all-gather.7 = f32[16,1,128]{2,1,0:T(1,128)S(1)} all-gather(f32[1,1,128]{2,1,0:T(1,128)S(1)} %bitcast.319), channel_id=3, replica_groups=mesh['tm_0'=4,'tm_1'=2,'docs'=16] {'docs'}, dimensions={0}, use_global_device_ids=true | all-gather | bytes 8704 | tf_op jit(solution)/shard_map/all_gather | solution.py:16
  31.4 16.3 %all-gather.6 = f32[16,1,128]{2,1,0:T(1,128)S(1)} all-gather(f32[1,1,128]{2,1,0:T(1,128)S(1)} %bitcast.318), channel_id=2, replica_groups=mesh['tm_0'=4,'tm_1'=2,'docs'=16] {'docs'}, dimensions={0}, use_global_device_ids=true | all-gather | bytes 8704 | tf_op jit(solution)/shard_map/all_gather | solution.py:16
  47.7 0.7 while.33
  48.4 2.2 fusion.53
  50.6 51.7 %all-gather.18.cloned.1.call-done = bf16[32768,128]{1,0:T(8,128)(2,1)} async-done(((bf16[2048,128]{1,0:T(8,128)(2,1)}), bf16[32768,128]{1,0:T(8,128)(2,1)}) %all-gather.18.cloned.1.call-update) | async-done | bytes 8388624 | tf_op jit(solution)/shard_map/all_gather | solution.py:112
  102.3 13.1 %fusion.62 = bf16[64,128]{1,0:T(8,128)(2,1)S(1)} fusion(bf16[32768,128]{1,0:T(8,128)(2,1)} %all-gather.18.cloned.1.call-done, s32[1,64,32768]{2,1,0:T(8,128)} %param.10, f32[1,64,128]{2,1,0:T(8,128)} %param.12, f32[128]{0:T(128)} %param.13), kind=kOutput, calls=%fused_computation.109 | convolution fusion | flops 1081925632 | bytes 16826880 | tf_op jit(solution)/shard_map/dot_general | solution.py:119
  115.4 12.6 %fusion.66 = bf16[64,128]{1,0:T(8,128)(2,1)S(1)} fusion(bf16[32768,128]{1,0:T(8,128)(2,1)} %all-gather.18.cloned.1.call-done, bf16[64,128]{1,0:T(8,128)(2,1)S(1)} %fusion.62, s32[1,64,32768]{2,1,0:T(8,128)} %param.10, f32[128]{0:T(128)S(1)} %copy-done.2), kind=kOutput, calls=%fused_computation.113 | convolution fusion | flops 1080680448 | bytes 16810496 | tf_op jit(solution)/shard_map/dot_general | solution.py:119
  128.0 12.4 %fusion.15 = f32[64,128]{1,0:T(8,128)S(1)} fusion(bf16[32768,128]{1,0:T(8,128)(2,1)} %all-gather.18.cloned.1.call-done, bf16[64,128]{1,0:T(8,128)(2,1)S(1)} %fusion.66, s32[1,64,32768]{2,1,0:T(8,128)} %param.10, f32[128]{0:T(128)S(1)} %copy-done.2), kind=kOutput, calls=%fused_computation.35 | convolution fusion | flops 1080057856 | bytes 16826880 | tf_op jit(solution)/shard_map/dot_general | solution.py:119
  140.4 9.2 %fusion.3 = bf16[64,32768]{1,0:T(8,128)(2,1)S(1)} fusion(bf16[32768,128]{1,0:T(8,128)(2,1)} %all-gather.18.cloned.1.call-done, s32[1,64,32768]{2,1,0:T(8,128)} %param.10, f32[64,128]{1,0:T(8,128)S(1)} %fusion.15), kind=kOutput, calls=%fused_computation.11 | convolution fusion | flops 543784960 | bytes 21004288 | tf_op jit(solution)/shard_map/dot_general | solution.py:115
  149.6 1.9 copy-done
  151.5 7.3 %fusion.2 = bf16[32768,128]{1,0:T(8,128)(2,1)} fusion(bf16[64,32768]{1,0:T(8,128)(2,1)S(1)} %fusion.3, bf16[32768,128]{1,0:T(8,128)(2,1)} %all-gather.18.cloned.1.call-done, f32[64,128]{1,0:T(8,128)S(1)} %fusion.15), kind=kOutput, calls=%fused_computation.9 | convolution fusion | flops 550076416 | bytes 21004288 | tf_op jit(solution)/shard_map/dot_general | solution.py:126
  158.9 0.5 copy-done.1
  159.5 7.0 %add_bitcast_fusion = (f32[1,64,128]{2,1,0:T(8,128)}, f32[128]{0:T(128)S(1)}) fusion(f32[128]{0:T(128)S(1)} %copy-done.2, bf16[64,32768]{1,0:T(8,128)(2,1)} %copy-done, bf16[32768,128]{1,0:T(8,128)(2,1)} %all-gather.18.cloned.1.call-done, f32[64,128]{1,0:T(8,128)S(1)} %fusion.15), kind=kOutput, calls=%fused_computation.129 | convolution fusion | flops 537526144 | bytes 12649472 | tf_op jit(solution)/shard_map/dot_general | solution.py:119
  166.6 67.0 %psum.7 = f32[8,128]{1,0:T(8,128)S(1)} all-reduce(f32[8,128]{1,0:T(8,128)S(1)} %broadcast_multiply_fusion), channel_id=1, replica_groups=mesh['tm_0'=4,'tm_1'=2,'docs'=16] {'tm_0','tm_1','docs'}, use_global_device_ids=true, to_apply=%region_5.6 | all-reduce | flops 1024 | bytes 8192 | tf_op jit(solution)/shard_map/psum | solution.py:138
  233.6 0.1 multiply_reduce_fusion
  233.8 0.9 while.34
  234.8 22.3 %reduce-scatter.2.cloned.1.call-done = bf16[2048,128]{1,0:T(8,128)(2,1)} async-done(((bf16[32768,128]{1,0:T(8,128)(2,1)}), bf16[2048,128]{1,0:T(8,128)(2,1)}) %reduce-scatter.2.cloned.1.call-update) | async-done | bytes 524304 | tf_op jit(solution)/shard_map/reduce_scatter | solution.py:123
  257.1 2.1 fusion.54
  259.3 4.6 %all-gather.10 = bf16[2,1,128]{2,1,0:T(2,128)(2,1)S(1)} all-gather(bf16[1,1,128]{2,1,0:T(2,128)(2,1)S(1)} %get-tuple-element.221), channel_id=5, replica_groups=mesh['tm_0'=4,'tm_1'=2,'docs'=16] {'tm_1'}, dimensions={0}, use_global_device_ids=true | all-gather | bytes 768 | tf_op jit(solution)/shard_map/all_gather | solution.py:38
  263.9 21.5 %all-gather.24.cloned.1.call-done = bf16[4096,128]{1,0:T(8,128)(2,1)} async-done(((bf16[2048,128]{1,0:T(8,128)(2,1)}), bf16[4096,128]{1,0:T(8,128)(2,1)}) %all-gather.24.cloned.1.call-update) | async-done | bytes 1048592 | tf_op jit(solution)/shard_map/all_gather | solution.py:38
  285.4 2.2 fusion.33
  287.7 7.9 %all-gather.11 = bf16[4,1,128]{2,1,0:T(2,128)(2,1)S(1)} all-gather(bf16[1,1,128]{2,1,0:T(2,128)(2,1)S(1)} %get-tuple-element.216), channel_id=1, replica_groups=mesh['tm_0'=4,'tm_1'=2,'docs'=16] {'tm_0'}, dimensions={0}, use_global_device_ids=true | all-gather | bytes 1280 | tf_op jit(solution)/shard_map/all_gather | solution.py:38
  295.6 22.6 %all-gather.20.cloned.1.call-done = bf16[4,2048,128]{2,1,0:T(8,128)(2,1)} async-done(((bf16[1,2048,128]{2,1,0:T(8,128)(2,1)}), bf16[4,2048,128]{2,1,0:T(8,128)(2,1)}) %all-gather.20.cloned.1.call-update) | async-done | bytes 2097168 | tf_op jit(solution)/shard_map/all_gather | solution.py:38
  318.2 3.9 %fusion.309 = (bf16[2048,128]{1,0:T(8,128)(2,1)}, f32[2048,128]{1,0:T(8,128)S(1)}) fusion(f32[128]{0:T(128)S(1)} %multiply_log_fusion, bf16[2048,128]{1,0:T(8,128)(2,1)} %reduce-scatter.2.cloned.1.call-done, f32[128]{0:T(128)S(1)} %get-tuple-element.175, pred[]{:T(512)S(6)} %gt.19, bf16[4096,128]{1,0:T(8,128)(2,1)} %all-gather.24.cloned.1.call-done, ...), kind=kLoop, calls=%fused_computation.345 | loop fusion | flops 8388608 | bytes 5248518 | tf_op jit(solution)/shard_map/convert_element_type | solution.py:59
  322.2 4.6 %all-gather.8 = bf16[2,1,128]{2,1,0:T(2,128)(2,1)S(1)} all-gather(bf16[1,1,128]{2,1,0:T(2,128)(2,1)S(1)} %get-tuple-element.218), channel_id=4, replica_groups=mesh['tm_0'=4,'tm_1'=2,'docs'=16] {'tm_1'}, dimensions={0}, use_global_device_ids=true | all-gather | bytes 768 | tf_op jit(solution)/shard_map/all_gather | solution.py:59
  326.8 20.7 %all-gather.26.cloned.1.call-done = bf16[4096,128]{1,0:T(8,128)(2,1)} async-done(((bf16[2048,128]{1,0:T(8,128)(2,1)}), bf16[4096,128]{1,0:T(8,128)(2,1)}) %all-gather.26.cloned.1.call-update) | async-done | bytes 1048592 | tf_op jit(solution)/shard_map/all_gather | solution.py:59
  347.5 2.2 fusion.37
  349.7 7.9 %all-gather.9 = bf16[4,1,128]{2,1,0:T(2,128)(2,1)S(1)} all-gather(bf16[1,1,128]{2,1,0:T(2,128)(2,1)S(1)} %get-tuple-element.212), channel_id=1, replica_groups=mesh['tm_0'=4,'tm_1'=2,'docs'=16] {'tm_0'}, dimensions={0}, use_global_device_ids=true | all-gather | bytes 1280 | tf_op jit(solution)/shard_map/all_gather | solution.py:59
  357.6 22.7 %all-gather.22.cloned.1.call-done = bf16[4,2048,128]{2,1,0:T(8,128)(2,1)} async-done(((bf16[1,2048,128]{2,1,0:T(8,128)(2,1)}), bf16[4,2048,128]{2,1,0:T(8,128)(2,1)}) %all-gather.22.cloned.1.call-update) | async-done | bytes 2097168 | tf_op jit(solution)/shard_map/all_gather | solution.py:59
  380.3 3.7 fusion.24
  (80 shorter events, 1.8 us)
Async XLA Ops:
  7.2 95.1 %all-gather.18.cloned.1.call-start = ((), (), s32[]{:S(2)}) async-start(), calls=%async_computation.1 | async-start | bytes 8912896 | tf_op jit(solution)/shard_map/all_gather | solution.py:112
  50.6 64.9 %copy-start.2 = (f32[128]{0:T(128)S(1)}, f32[128]{0:T(128)}, u32[]{:S(2)}) copy-start(f32[128]{0:T(128)} %param.13) | copy-start | bytes 1540
  50.6 206.5 %reduce-scatter.2.cloned.1.call-start = ((), (), s32[]{:S(2)}) async-start(), calls=%async_computation.2 | async-start | bytes 8912896 | tf_op jit(solution)/shard_map/reduce_scatter | solution.py:123
  149.6 1.9 copy-start
  158.8 0.7 copy-start.1
  158.9 126.5 %all-gather.24.cloned.1.call-start = ((), (), s32[]{:S(2)}) async-start(), calls=%async_computation.5 | async-start | bytes 1572864 | tf_op jit(solution)/shard_map/all_gather | solution.py:38
  159.5 74.2 %copy-start.3 = (f32[128]{0:T(128)S(1)}, f32[128]{0:T(128)}, u32[]{:S(2)}) copy-start(f32[128]{0:T(128)} %param.15) | copy-start | bytes 1540
  159.5 75.2 %copy-start.4 = (pred[8]{0:T(512)(128)(4,1)S(1)}, pred[8]{0:T(512)(128)(4,1)}, u32[]{:S(2)}) copy-start(pred[8]{0:T(512)(128)(4,1)} %constant.117.clone.1) | copy-start | bytes 28
  259.2 59.0 %all-gather.20.cloned.1.call-start = ((), (), s32[]{:S(2)}) async-start(), calls=%async_computation.3 | async-start | bytes 2621440 | tf_op jit(solution)/shard_map/all_gather | solution.py:38
  287.6 59.9 %all-gather.26.cloned.1.call-start = ((), (), s32[]{:S(2)}) async-start(), calls=%async_computation.6 | async-start | bytes 1572864 | tf_op jit(solution)/shard_map/all_gather | solution.py:59
  322.2 58.1 %all-gather.22.cloned.1.call-start = ((), (), s32[]{:S(2)}) async-start(), calls=%async_computation.4 | async-start | bytes 2621440 | tf_op jit(solution)/shard_map/all_gather | solution.py:59
Sparse Core Ops, SparseCore 0:
  50.7 51.5 all-gather.17
  159.0 98.0 reduce-scatter.1
  259.3 26.0 all-gather.23
  287.7 30.4 all-gather.19
  322.3 25.1 all-gather.25
  349.8 30.4 all-gather.21
where the time goes:
time: 391 us
  waiting for transfers between devices  162 us (41%)
  blocking collectives  129 us (33%)
  matrix products  61.6 us (16%)
  other arithmetic  20.3 us (5%)
  between operations  14.3 us (4%)
    psum x1, blocking collectives, body(): totals = lax.psum(placed, TM_DOCS)  67 us
    all_gather x1, waiting for transfers between devices, body(): beta_full = lax.all_gather(beta_slab, 'docs', axis=0, tiled=True)  51.7 us
    dot_general x4, matrix products, body(): jnp.dot(ratios, beta_full, preferred_element_type=jnp.float32)  45.1 us
    all_gather x2, waiting for transfers between devices, carried_in(): lax.all_gather(part.astype(kind), axis)  44.2 us
    all_gather x2, waiting for transfers between devices, prefix_by_axis(): lax.all_gather(part.astype(kind), axis)  43.4 us
    all_gather x2, blocking collectives, merged(): gathered = jax.tree.map(lambda a: lax.all_gather(a, axis), part)  37.5 us
    reduce_scatter x1, waiting for transfers between devices, body(): lax.psum_scatter((beta_full.astype(jnp.float32) * lax.dot_general(ratios,...  22.3 us
    all_gather x2, blocking collectives, carried_in(): lax.all_gather(part.astype(kind), axis)  12.5 us
  transfers between devices with their start and end apart: 6, of which 6 were waited for; matrix products, arithmetic and copies ran while one was open for 2% of the time, Pallas kernels for 0%

commit v1 on v0

--- a/solution.py
+++ b/solution.py
@@ -135,7 +135,7 @@
     slices = lax.axis_size(TM)
     own_row = (jnp.arange(slices) == slice_index).astype(jnp.float32)
     placed = own_row[:, None] * jnp.sum(update, axis=0)[None, :]
-    totals = lax.psum(placed, TM_DOCS)
+    totals = jnp.sum(lax.all_gather(placed, TM_DOCS), axis=0)
     gains, smooth = chain_factors(totals, chain_var, obs_noise)
     own_total = jnp.sum(own_row[:, None] * totals, axis=0)
     own_gain = jnp.sum(own_row[:, None] * gains, axis=0)

time: 391 us -> 473 us (1.21)
  blocking collectives: 129 us -> 241 us
  waiting for transfers between devices: 162 us -> 131 us
    all_gather x0 -> x1, blocking collectives: none -> 178 us  [body(): totals = jnp.sum(lax.all_gather(placed, TM_DOCS), axis=0)]
    psum x1 -> x0, blocking collectives: 67 us -> none  [body(): totals = lax.psum(placed, TM_DOCS)]
    reduce_scatter x1, waiting for transfers between devices: 22.3 us -> 0.01 us  [body(): lax.psum_scatter((beta_full.astype(jnp.float32) * lax.dot_general(ratios,...]
    all_gather x2, waiting for transfers between devices: 44.2 us -> 36.3 us  [carried_in(): lax.all_gather(part.astype(kind), axis)]
  transfers between devices with their start and end apart: 6 -> 6, of which waited for: 6 -> 5; matrix products, arithmetic and copies ran while one was open for 2% -> 2% of each run, Pallas kernels for 0% -> 0%
where the time goes in v1:
time: 473 us; the launch traced here: 472 us
  blocking collectives  241 us (51%)
  waiting for transfers between devices  131 us (28%)
  matrix products  61.6 us (13%)
  other arithmetic  20.4 us (4%)
  between operations  14.3 us (3%)
    all_gather x1, blocking collectives, body(): totals = jnp.sum(lax.all_gather(placed, TM_DOCS), axis=0)  178 us
    all_gather x1, waiting for transfers between devices, body(): beta_full = lax.all_gather(beta_slab, 'docs', axis=0, tiled=True)  51.7 us
    dot_general x4, matrix products, body(): jnp.dot(ratios, beta_full, preferred_element_type=jnp.float32)  45.1 us
    all_gather x2, waiting for transfers between devices, prefix_by_axis(): lax.all_gather(part.astype(kind), axis)  43.4 us
    all_gather x2, blocking collectives, merged(): gathered = jax.tree.map(lambda a: lax.all_gather(a, axis), part)  37.5 us
    all_gather x2, waiting for transfers between devices, carried_in(): lax.all_gather(part.astype(kind), axis)  36.3 us
    all_gather x2, blocking collectives, carried_in(): lax.all_gather(part.astype(kind), axis)  12.5 us
    all_gather x2, blocking collectives, prefix_by_axis(): lax.all_gather(part.astype(kind), axis)  12.5 us
  transfers between devices with their start and end apart: 6, of which 5 were waited for; matrix products, arithmetic and copies ran while one was open for 2% of the time, Pallas kernels for 0%

profile of v1, /device:TPU:1, one launch (start us, length us, event | category | flops | bytes accessed | tf_op | source)
XLA Modules:
  0.0 472.4 jit_solution(16370321237339746659)
XLA Ops:
  7.2 1.5 reduce_max.9
  8.7 1.5 fusion.51
  10.2 21.2 %all-gather.6 = f32[16,1,128]{2,1,0:T(1,128)S(1)} all-gather(f32[1,1,128]{2,1,0:T(1,128)S(1)} %bitcast.318), channel_id=2, replica_groups=mesh['tm_0'=4,'tm_1'=2,'docs'=16] {'docs'}, dimensions={0}, use_global_device_ids=true | all-gather | bytes 8704 | tf_op jit(solution)/shard_map/all_gather | solution.py:16
  31.4 16.3 %all-gather.7 = f32[16,1,128]{2,1,0:T(1,128)S(1)} all-gather(f32[1,1,128]{2,1,0:T(1,128)S(1)} %bitcast.319), channel_id=3, replica_groups=mesh['tm_0'=4,'tm_1'=2,'docs'=16] {'docs'}, dimensions={0}, use_global_device_ids=true | all-gather | bytes 8704 | tf_op jit(solution)/shard_map/all_gather | solution.py:16
  47.7 0.7 while.33
  48.4 2.2 fusion.53
  50.6 51.7 %all-gather.18.cloned.1.call-done = bf16[32768,128]{1,0:T(8,128)(2,1)} async-done(((bf16[2048,128]{1,0:T(8,128)(2,1)}), bf16[32768,128]{1,0:T(8,128)(2,1)}) %all-gather.18.cloned.1.call-update) | async-done | bytes 8388624 | tf_op jit(solution)/shard_map/all_gather | solution.py:112
  102.3 13.1 %fusion.62 = bf16[64,128]{1,0:T(8,128)(2,1)S(1)} fusion(bf16[32768,128]{1,0:T(8,128)(2,1)} %all-gather.18.cloned.1.call-done, s32[1,64,32768]{2,1,0:T(8,128)} %param.10, f32[1,64,128]{2,1,0:T(8,128)} %param.12, f32[128]{0:T(128)} %param.13), kind=kOutput, calls=%fused_computation.109 | convolution fusion | flops 1081925632 | bytes 16826880 | tf_op jit(solution)/shard_map/dot_general | solution.py:119
  115.4 12.6 %fusion.66 = bf16[64,128]{1,0:T(8,128)(2,1)S(1)} fusion(bf16[32768,128]{1,0:T(8,128)(2,1)} %all-gather.18.cloned.1.call-done, bf16[64,128]{1,0:T(8,128)(2,1)S(1)} %fusion.62, s32[1,64,32768]{2,1,0:T(8,128)} %param.10, f32[128]{0:T(128)S(1)} %copy-done.2), kind=kOutput, calls=%fused_computation.113 | convolution fusion | flops 1080680448 | bytes 16810496 | tf_op jit(solution)/shard_map/dot_general | solution.py:119
  128.0 12.4 %fusion.15 = f32[64,128]{1,0:T(8,128)S(1)} fusion(bf16[32768,128]{1,0:T(8,128)(2,1)} %all-gather.18.cloned.1.call-done, bf16[64,128]{1,0:T(8,128)(2,1)S(1)} %fusion.66, s32[1,64,32768]{2,1,0:T(8,128)} %param.10, f32[128]{0:T(128)S(1)} %copy-done.2), kind=kOutput, calls=%fused_computation.35 | convolution fusion | flops 1080057856 | bytes 16826880 | tf_op jit(solution)/shard_map/dot_general | solution.py:119
  140.4 9.2 %fusion.3 = bf16[64,32768]{1,0:T(8,128)(2,1)S(1)} fusion(bf16[32768,128]{1,0:T(8,128)(2,1)} %all-gather.18.cloned.1.call-done, s32[1,64,32768]{2,1,0:T(8,128)} %param.10, f32[64,128]{1,0:T(8,128)S(1)} %fusion.15), kind=kOutput, calls=%fused_computation.11 | convolution fusion | flops 543784960 | bytes 21004288 | tf_op jit(solution)/shard_map/dot_general | solution.py:115
  149.6 1.9 copy-done
  151.5 7.3 %fusion.2 = bf16[32768,128]{1,0:T(8,128)(2,1)} fusion(bf16[64,32768]{1,0:T(8,128)(2,1)S(1)} %fusion.3, bf16[32768,128]{1,0:T(8,128)(2,1)} %all-gather.18.cloned.1.call-done, f32[64,128]{1,0:T(8,128)S(1)} %fusion.15), kind=kOutput, calls=%fused_computation.9 | convolution fusion | flops 550076416 | bytes 21004288 | tf_op jit(solution)/shard_map/dot_general | solution.py:126
  158.9 0.5 copy-done.1
  159.5 7.0 %add_bitcast_fusion = (f32[1,64,128]{2,1,0:T(8,128)}, f32[128]{0:T(128)S(1)}) fusion(f32[128]{0:T(128)S(1)} %copy-done.2, bf16[64,32768]{1,0:T(8,128)(2,1)} %copy-done, bf16[32768,128]{1,0:T(8,128)(2,1)} %all-gather.18.cloned.1.call-done, f32[64,128]{1,0:T(8,128)S(1)} %fusion.15), kind=kOutput, calls=%fused_computation.129 | convolution fusion | flops 537526144 | bytes 12649472 | tf_op jit(solution)/shard_map/dot_general | solution.py:119
  166.6 178.5 %all_gather.60 = f32[128,8,128]{2,1,0:T(8,128)S(1)} all-gather(f32[1,8,128]{2,1,0:T(8,128)S(1)} %broadcast_multiply_fusion), channel_id=1, replica_groups=mesh['tm_0'=4,'tm_1'=2,'docs'=16] {'tm_0','tm_1','docs'}, dimensions={0}, use_global_device_ids=true | all-gather | bytes 528384 | tf_op jit(solution)/shard_map/all_gather | solution.py:138
  345.1 0.2 fusion.309
  345.4 0.8 while.34
  346.3 0.1 fusion.192
  346.4 2.1 fusion.54
  348.5 4.6 all-gather.10
  353.1 13.7 %all-gather.24.cloned.1.call-done = bf16[4096,128]{1,0:T(8,128)(2,1)} async-done(((bf16[2048,128]{1,0:T(8,128)(2,1)}), bf16[4096,128]{1,0:T(8,128)(2,1)}) %all-gather.24.cloned.1.call-update) | async-done | bytes 1048592 | tf_op jit(solution)/shard_map/all_gather | solution.py:38
  366.9 2.2 fusion.33
  369.1 7.9 %all-gather.11 = bf16[4,1,128]{2,1,0:T(2,128)(2,1)S(1)} all-gather(bf16[1,1,128]{2,1,0:T(2,128)(2,1)S(1)} %get-tuple-element.217), channel_id=1, replica_groups=mesh['tm_0'=4,'tm_1'=2,'docs'=16] {'tm_0'}, dimensions={0}, use_global_device_ids=true | all-gather | bytes 1280 | tf_op jit(solution)/shard_map/all_gather | solution.py:38
  377.0 22.6 %all-gather.20.cloned.1.call-done = bf16[4,2048,128]{2,1,0:T(8,128)(2,1)} async-done(((bf16[1,2048,128]{2,1,0:T(8,128)(2,1)}), bf16[4,2048,128]{2,1,0:T(8,128)(2,1)}) %all-gather.20.cloned.1.call-update) | async-done | bytes 2097168 | tf_op jit(solution)/shard_map/all_gather | solution.py:38
  399.7 3.9 fusion.310
  403.7 4.6 all-gather.8
  408.3 20.7 %all-gather.26.cloned.1.call-done = bf16[4096,128]{1,0:T(8,128)(2,1)} async-done(((bf16[2048,128]{1,0:T(8,128)(2,1)}), bf16[4096,128]{1,0:T(8,128)(2,1)}) %all-gather.26.cloned.1.call-update) | async-done | bytes 1048592 | tf_op jit(solution)/shard_map/all_gather | solution.py:59
  429.0 2.2 fusion.37
  431.2 7.9 %all-gather.9 = bf16[4,1,128]{2,1,0:T(2,128)(2,1)S(1)} all-gather(bf16[1,1,128]{2,1,0:T(2,128)(2,1)S(1)} %get-tuple-element.213), channel_id=1, replica_groups=mesh['tm_0'=4,'tm_1'=2,'docs'=16] {'tm_0'}, dimensions={0}, use_global_device_ids=true | all-gather | bytes 1280 | tf_op jit(solution)/shard_map/all_gather | solution.py:59
  439.1 22.7 %all-gather.22.cloned.1.call-done = bf16[4,2048,128]{2,1,0:T(8,128)(2,1)} async-done(((bf16[1,2048,128]{2,1,0:T(8,128)(2,1)}), bf16[4,2048,128]{2,1,0:T(8,128)(2,1)}) %all-gather.22.cloned.1.call-update) | async-done | bytes 2097168 | tf_op jit(solution)/shard_map/all_gather | solution.py:59
  461.8 3.7 fusion.24
  (80 shorter events, 1.7 us)
Async XLA Ops:
  7.2 95.1 %all-gather.18.cloned.1.call-start = ((), (), s32[]{:S(2)}) async-start(), calls=%async_computation.1 | async-start | bytes 8912896 | tf_op jit(solution)/shard_map/all_gather | solution.py:112
  50.6 64.9 %copy-start.2 = (f32[128]{0:T(128)S(1)}, f32[128]{0:T(128)}, u32[]{:S(2)}) copy-start(f32[128]{0:T(128)} %param.13) | copy-start | bytes 1540
  50.6 295.8 %reduce-scatter.2.cloned.1.call-start = ((), (), s32[]{:S(2)}) async-start(), calls=%async_computation.2 | async-start | bytes 8912896 | tf_op jit(solution)/shard_map/reduce_scatter | solution.py:123
  149.6 1.9 copy-start
  158.8 0.7 copy-start.1
  158.8 208.0 %all-gather.24.cloned.1.call-start = ((), (), s32[]{:S(2)}) async-start(), calls=%async_computation.5 | async-start | bytes 1572864 | tf_op jit(solution)/shard_map/all_gather | solution.py:38
  159.5 185.8 %copy-start.3 = (f32[128]{0:T(128)S(1)}, f32[128]{0:T(128)}, u32[]{:S(2)}) copy-start(f32[128]{0:T(128)} %param.15) | copy-start | bytes 1540
  159.5 186.8 %copy-start.4 = (pred[8]{0:T(512)(128)(4,1)S(1)}, pred[8]{0:T(512)(128)(4,1)}, u32[]{:S(2)}) copy-start(pred[8]{0:T(512)(128)(4,1)} %constant.117.clone.1) | copy-start | bytes 28
  348.5 51.2 %all-gather.20.cloned.1.call-start = ((), (), s32[]{:S(2)}) async-start(), calls=%async_computation.3 | async-start | bytes 2621440 | tf_op jit(solution)/shard_map/all_gather | solution.py:38
  369.1 59.9 %all-gather.26.cloned.1.call-start = ((), (), s32[]{:S(2)}) async-start(), calls=%async_computation.6 | async-start | bytes 1572864 | tf_op jit(solution)/shard_map/all_gather | solution.py:59
  403.6 58.1 %all-gather.22.cloned.1.call-start = ((), (), s32[]{:S(2)}) async-start(), calls=%async_computation.4 | async-start | bytes 2621440 | tf_op jit(solution)/shard_map/all_gather | solution.py:59
Sparse Core Ops, SparseCore 0:
  50.7 51.5 all-gather.17
  159.0 99.7 reduce-scatter.1
  348.6 18.2 all-gather.23
  369.2 30.4 all-gather.19
  403.8 25.1 all-gather.25
  431.3 30.4 all-gather.21
